TPU v7x, 128 devices: a whole 4x4x4 slice. The times are simulated.
128 devices in a mesh: lat: 8 (over z, core), lon: 16 (over y, x).
Axes of the slice: x: 4, y: 4, z: 4, core: 2. Of those that a mesh axis runs over, the one named last changes fastest.
Arguments:
- winds: bfloat16 [32, 64, 3, 40, 128], P('lat', 'lon'), may hold values from -6 to 6
- positions: float32 [16384, 3, 128], P(('lat', 'lon')), may hold values from 0 to 39, as said below
- velocity: float32 [16384, 3, 128], P(('lat', 'lon')), may hold values from -6 to 6
- increments: float32 [16384, 3, 128], P(('lat', 'lon')), may hold values from -6 to 6
- mass: float32 [16384, 8, 128], P(('lat', 'lon')), may hold values from 0.1 to 1
- requests: int32 [128, 128, 2], P(('lat', 'lon')), may hold values from 0 to 15
- block_slots: int32 [16384, 1], P(('lat', 'lon')), may hold values from 0 to 255; in each aligned block of 128 rows (0 to 127, 128 to 255, ...) at most 2 rows name the same one
- destinations: int32 [16384, 1], P(('lat', 'lon')), may hold values from 0 to 127; in each aligned block of 128 rows (0 to 127, 128 to 255, ...) at most 2 rows name the same one
- cell_keys: int32 [16384, 128], P(('lat', 'lon')), may hold values from 0 to 2047, as said below
Outputs:
- moved: float32 [16384, 3, 128], P(('lat', 'lon'))
- turbulence: float32 [16384, 3, 128], P(('lat', 'lon'))
- concentration: float32 [32, 64, 8, 40, 128], P('lat', 'lon')
Inputs may be any that keep to these rules, and one draw needn't show every extreme that they name: `positions`: component 0 (cell row) lies in 0 to 7, component 1 (cell column) in 0 to 15, component 2 (level) in 0 to 39. requests[o, t, k] names a met block of tile t by its local number. `block_slots`: slot k stands for the (k % 2)-th request that the owner sends to tile k // 2; of the 128 blocks of one owner at most 2 have the same slot, and on some owners one slot gets exactly 2. `destinations`: of the 128 blocks of one owner at most 2 have the same destination; on some owners one destination gets exactly 2. `cell_keys`: a key is (local met block) * 128 + cell of the destination tile; all keys of one particle block lie in one met block.
All inputs are finite; a program needn't handle non-finite values.
Results may differ from a plain program's by a relative error of at most 0.0027.
Values may be sent and summed in bfloat16 or wider, within the bound.
No kernel may reach another device: no remote copies, remote signals or barrier semaphores. Data moves between devices by JAX's collectives and lax.ppermute only.
A program may use at most 64 MiB of HBM per device.

v0:
```python
import jax
import jax.numpy as jnp
from jax import lax
from jax.experimental import pallas as pl
from jax.experimental.pallas import tpu as pltpu
from jax.sharding import PartitionSpec as P

BY = 8
BX = 16
MBC = 128
LEV = 40
S = 8
BLK = 128
MB = 16
Q = 2
CAP = 2
ROOM = Q * CAP

DECAY = 0.8
KICK = 0.6
STEP = 0.5

AXES = ("lat", "lon")
LOW16 = 0xFFFF
ROW_SCALE = 65535.0 / (BY - 1)
COL_SCALE = 65535.0 / (BX - 1)
LEV_SCALE = 65535.0 / (LEV - 1)
Z_ONE = float(1 << 22)
W_TOP = 6.1
W_SCALE = 65535.0 / (2 * W_TOP)
M_SCALE = 32767.0
SAMPLE_UNROLL = 12
PAIR_UNROLL = 16

SHARE_ROW = 2 * ROOM
NOTE_ROW = SHARE_ROW + CAP * S // 2
ROWS = NOTE_ROW + 1
WIND_ROWS = ROOM + ROOM // 2
HOME_AT = ROOM
LANDED_AT = HOME_AT + CAP
TAKEN_AT = LANDED_AT + 1
EACH = 8
PLAN = 1024
HOMES_AT = 576
PAIRS_AT = PLAN - 1


def hat(offset):
    return jnp.maximum(0.0, 1.0 - jnp.abs(offset))


def fixed(value, scale, shift=0.0):
    return ((value + shift) * scale + 0.5).astype(jnp.int32)


def upper(word):
    return lax.shift_right_logical(word, jnp.int32(16)).astype(jnp.float32)


def lower(word):
    return (word & LOW16).astype(jnp.float32)


def whole(space=pltpu.VMEM):
    return pl.BlockSpec(memory_space=space)


def read_notes(box, rows, notes, sem):
    devices = notes.shape[1]
    sent = box[pl.ds(NOTE_ROW, devices, stride=ROWS), :].astype(jnp.float32)
    rows[...] = sent.T[0 : notes.shape[0], :].astype(jnp.int32)
    copy = pltpu.make_async_copy(rows, notes, sem)
    copy.start()
    copy.wait()


def pack_kernel(
    slots_hbm, asked_hbm, targets_hbm, keys_hbm, pos_hbm, mass_hbm,
    box, places,
    slots, asked, targets, keys, pos, mass, spots, ranks, sems,
):
    blocks, devices = mass.shape[0], asked.shape[1]
    copies = [
        pltpu.make_async_copy(src, dst, sems.at[i])
        for i, (src, dst) in enumerate(
            (
                (slots_hbm, slots),
                (targets_hbm, targets),
                (asked_hbm, asked),
                (keys_hbm, keys),
                (pos_hbm, pos),
                (mass_hbm, mass),
            )
        )
    ]
    for copy in copies:
        copy.start()
    square = (blocks, blocks)
    down = lax.broadcasted_iota(jnp.int32, square, 0)
    along = lax.broadcasted_iota(jnp.int32, square, 1)

    def stand(row):
        return jnp.broadcast_to(row.astype(jnp.float32), square).T.astype(jnp.int32)

    def rank(row):
        same = (stand(row) == row) & (down < along)
        return jnp.sum(jnp.where(same, 1.0, 0.0), axis=0, keepdims=True).astype(jnp.int32)

    copies[0].wait()
    slot = slots[...]
    tile = slot // Q
    order = rank(tile)
    lons = lax.axis_size("lon")
    core = (tile // lons) % 2
    helper = (order + lax.axis_index("lat") + lax.axis_index("lon")) % 2
    host = tile + (helper - core) * lons
    seat = core * (ROOM // 2) + order // 2
    copies[1].wait()
    target = targets[...]
    turn = rank(target)
    ranks[0:1, :] = host * ROWS + 2 * seat
    ranks[1:2, :] = target * ROWS + SHARE_ROW + turn * (S // 2)
    ranks[2:3, :] = host * WIND_ROWS + seat
    ranks[3:4, :] = host * WIND_ROWS + ROOM + seat // 2
    ranks[4:5, :] = 16 - 16 * (seat % 2)
    ranks[5:6, :] = target * CAP + turn
    ranked = pltpu.make_async_copy(ranks, places, sems.at[len(copies)])
    ranked.start()
    slot_down = stand(slot)
    tile_down = slot_down // Q
    copies[2].wait()
    met = jnp.where(slot_down % Q == 0, asked[0:1, :], asked[1:2, :])
    met = jnp.where(tile_down == along, met, 0).astype(jnp.float32)
    met = jnp.sum(met, axis=1, keepdims=True)
    met = met + jnp.where(stand(helper) == stand(core), 0.0, float(MB))
    copies[3].wait()
    home = (keys[:, 0:1] // MBC).astype(jnp.float32)
    said = jnp.where(along == stand(seat), met, 0.0)
    said = jnp.where(along == TAKEN_AT, jnp.where(stand(core) == 0, 1.0, float(EACH)), said)
    more = jnp.where(along == HOME_AT + stand(turn), home, 0.0) + jnp.where(
        along == LANDED_AT, 1.0, 0.0
    )
    mine = jnp.concatenate([down == host, down == target], axis=1)
    notes = jnp.dot(
        jnp.where(mine, 1.0, 0.0).astype(jnp.bfloat16),
        jnp.concatenate([said, more], axis=0).astype(jnp.bfloat16),
        preferred_element_type=jnp.float32,
    )
    box[pl.ds(NOTE_ROW, devices, stride=ROWS), :] = notes.astype(jnp.int32)
    copies[4].wait()
    spots[pl.ds(0, blocks, stride=2), :] = (fixed(pos[0], ROW_SCALE) << 16) | fixed(
        pos[1], COL_SCALE
    )
    spots[pl.ds(1, blocks, stride=2), :] = (pos[2] * Z_ONE).astype(jnp.int32)
    copies[5].wait()
    ranked.wait()

    def put(b, _):
        box[pl.ds(places[0, b], 2), :] = spots[pl.ds(2 * b, 2), :]
        share = fixed(mass[b], M_SCALE)
        box[pl.ds(places[1, b], S // 2), :] = (share[0 : S // 2] << 16) | share[S // 2 :]
        return 0

    lax.fori_loop(0, blocks, put, 0, unroll=8)


def sample_kernel(box, winds, out, queue, found, rows, notes, sem):
    devices = notes.shape[1]
    read_notes(box, rows, notes, sem)

    def enlist(t, n):
        taken = notes[TAKEN_AT, t]
        for r in range(ROOM // 2):
            queue[n + r] = t * ROOM + r
        n = n + taken % EACH
        for r in range(ROOM // 2):
            queue[n + r] = t * ROOM + ROOM // 2 + r
        return n + taken // EACH

    n = lax.fori_loop(0, devices, enlist, 0, unroll=4)
    levels = lax.broadcasted_iota(jnp.int32, (LEV, BLK), 0).astype(jnp.float32)
    lats = lax.broadcasted_iota(jnp.int32, (BY, BLK), 0).astype(jnp.float32)
    lons = lax.broadcasted_iota(jnp.int32, (BX, BLK), 0).astype(jnp.float32)

    def step(i, _):
        for j in range(SAMPLE_UNROLL):
            item = queue[jnp.minimum(i * SAMPLE_UNROLL + j, n - 1)]
            row = (item // ROOM) * ROWS + 2 * (item % ROOM)
            yx = box[pl.ds(row, 1), :]
            height = box[pl.ds(row + 1, 1), :]
            hy = hat(upper(yx) * (1.0 / ROW_SCALE) - lats)
            hx = hat(lower(yx) * (1.0 / COL_SCALE) - lons)
            wz = hat(height.astype(jnp.float32) * (1.0 / Z_ONE) - levels)
            wz = wz.astype(jnp.bfloat16).astype(jnp.float32)
            flat = (hy[:, None, :] * hx[None, :, :]).reshape(MBC, BLK)
            high = flat.astype(jnp.bfloat16)
            low = (flat - high.astype(jnp.float32)).astype(jnp.bfloat16)
            met = winds[notes[item % ROOM, item // ROOM]]
            level_wind = jnp.dot(met, high, preferred_element_type=jnp.float32) + jnp.dot(
                met, low, preferred_element_type=jnp.float32
            )
            wind = [
                jnp.sum(level_wind[c * LEV : (c + 1) * LEV] * wz, axis=0, keepdims=True)
                for c in range(3)
            ]
            found[pl.ds(2 * item, 1), :] = (fixed(wind[0], W_SCALE, W_TOP) << 16) | fixed(
                wind[1], W_SCALE, W_TOP
            )
            found[pl.ds(2 * item + 1, 1), :] = fixed(wind[2], W_SCALE, W_TOP)
        return 0

    lax.fori_loop(0, pl.cdiv(n, SAMPLE_UNROLL), step, 0)

    def every(r):
        return found[pl.ds(r, devices, stride=2 * ROOM), :]

    for r in range(ROOM):
        out[pl.ds(r, devices, stride=WIND_ROWS), :] = every(2 * r)
    for r in range(0, ROOM, 2):
        out[pl.ds(ROOM + r // 2, devices, stride=WIND_ROWS), :] = (every(2 * r + 1) << 16) | (
            every(2 * r + 3) & LOW16
        )


def order_kernel(box, plan, shares, rows, notes, starts, tally, sem):
    devices = notes.shape[1]
    read_notes(box, rows, notes, sem)

    room = shares.shape[0] // S

    def clear(i, _):
        plan[i] = -1
        return 0

    lax.fori_loop(0, room, clear, 0, unroll=8)

    def clear_home(i, _):
        plan[HOMES_AT + i] = 0
        return 0

    lax.fori_loop(0, room // 2, clear_home, 0, unroll=8)
    for h in range(MB):
        tally[h] = 0

    def tell(t, _):
        landed = notes[LANDED_AT, t]
        for r in range(CAP):
            home = jnp.where(r < landed, notes[HOME_AT + r, t], MB)
            tally[home] = tally[home] + 1
        return 0

    tally[MB] = 0
    lax.fori_loop(0, devices, tell, 0, unroll=4)
    n = jnp.int32(0)
    for h in range(MB):
        starts[h] = n
        n = n + (tally[h] + 1) // 2 * 2
    starts[MB] = room

    def place(t, _):
        landed = notes[LANDED_AT, t]
        for r in range(CAP):
            there = r < landed
            home = jnp.where(there, notes[HOME_AT + r, t], MB)
            at = starts[home]
            starts[home] = at + 1
            plan[at] = jnp.where(there, t * CAP + r, -1)
            plan[HOMES_AT + at // 2] = jnp.where(there, home, 0)
        return 0

    lax.fori_loop(0, devices, place, 0, unroll=4)
    plan[PAIRS_AT] = n // 2

    def expand(i, _):
        for j in range(2 * PAIR_UNROLL):
            at = i * 2 * PAIR_UNROLL + j
            item = plan[at]
            row = jnp.maximum(item, 0)
            packed = box[pl.ds((row // CAP) * ROWS + SHARE_ROW + (row % CAP) * (S // 2), S // 2), :]
            unit = jnp.where(item < 0, 0.0, 1.0 / M_SCALE)
            shares[pl.ds(S * at, S), :] = (
                jnp.concatenate([upper(packed), lower(packed)], axis=0) * unit
            )
        return 0

    lax.fori_loop(0, jnp.maximum(pl.cdiv(n, 2 * PAIR_UNROLL), 1), expand, 0)


def advance(pos, vel, noise, word, top):
    wind = word * (1.0 / W_SCALE) - W_TOP
    fresh = DECAY * vel + KICK * noise
    return fresh, jnp.clip(pos + STEP * (wind + fresh), 0.0, top)


def take_up(places, box, z_rows):
    def take(b, _):
        z_rows[pl.ds(b, 1), :] = lax.shift_right_logical(
            box[pl.ds(places[3, b], 1), :], jnp.full((1, BLK), places[4, b], jnp.int32)
        )
        return 0

    lax.fori_loop(0, z_rows.shape[0], take, 0, unroll=8)
    return lower(z_rows[...])


def height_kernel(places, plan, box, pos, vel, noise, keys, out, z_rows):
    up = take_up(places, box, z_rows)
    _, height = advance(pos[2], vel[2], noise[2], up, LEV - 1.0)
    z_rows[...] = (keys[...] << 16) | fixed(height, LEV_SCALE)

    def put(b, _):
        out[pl.ds(places[5, b], 1), :] = z_rows[pl.ds(b, 1), :]
        return 0

    lax.fori_loop(0, z_rows.shape[0], put, 0, unroll=8)


def move_kernel(places, box, pos, vel, noise, moved, turb, yx_rows, z_rows):
    def take(b, _):
        yx_rows[pl.ds(b, 1), :] = box[pl.ds(places[2, b], 1), :]
        return 0

    lax.fori_loop(0, yx_rows.shape[0], take, 0, unroll=8)
    yx = yx_rows[...]
    words = (upper(yx), lower(yx), take_up(places, box, z_rows))
    for c, top in enumerate((BY - 1.0, BX - 1.0, LEV - 1.0)):
        turb[c], moved[c] = advance(pos[c], vel[c], noise[c], words[c], top)


def deposit_kernel(plan, box, shares, out, total, sems):
    n = plan[PAIRS_AT]
    total[...] = jnp.zeros(total.shape, jnp.float32)
    level = lax.broadcasted_iota(jnp.int32, (8, BLK), 0).astype(jnp.float32)
    cells = lax.broadcasted_iota(jnp.int32, (MBC, BLK), 0).astype(jnp.float32)
    cells = cells.astype(jnp.bfloat16)
    one, none = jnp.bfloat16(1), jnp.bfloat16(0)

    def step(i, done):
        for j in range(PAIR_UNROLL):
            pair = i * PAIR_UNROLL + j
            weights, picks = [], []
            for half in range(2):
                at = 2 * pair + half
                row = jnp.maximum(plan[at], 0)
                word = box[pl.ds(row, 1), :]
                height = jnp.broadcast_to(lower(word) * (1.0 / LEV_SCALE), (8, BLK))
                vert = [hat(height - (level + 8.0 * k)) for k in range(LEV // 8)]
                held = [
                    shares[pl.ds(S * at + s, 8, stride=0), :] * part for s in range(S) for part in vert
                ]
                weights.append(jnp.concatenate(held, axis=0).astype(jnp.bfloat16))
                cell = (word >> 16) & (MBC - 1)
                cell = cell.astype(jnp.float32).astype(jnp.bfloat16)
                picks.append(jnp.where(cells == cell, one, none))
            part = lax.dot_general(
                jnp.concatenate(weights, axis=1),
                jnp.concatenate(picks, axis=1),
                (((1,), (1,)), ((), ())),
                preferred_element_type=jnp.float32,
            )
            home = plan[HOMES_AT + pair]
            total[home] = total[home] + part
        later = (i + 1) * PAIR_UNROLL
        final = jnp.where(later < n, plan[HOMES_AT + later], MB)

        def leave(h, _):
            pltpu.make_async_copy(total.at[h], out.at[h], sems.at[h]).start()
            return 0

        lax.fori_loop(done, final, leave, 0)
        return final

    steps = jnp.maximum(pl.cdiv(n, PAIR_UNROLL), 1)
    lax.fori_loop(0, steps, step, jnp.int32(0))
    for h in range(MB):
        pltpu.make_async_copy(total.at[h], out.at[h], sems.at[h]).wait()


def swap(box, devices):
    rows = box.shape[0] // devices
    step = 8 if rows % 8 == 0 else 2 if rows % 2 == 0 else 1
    whole_box = box.reshape(devices * rows // step, step, BLK)
    arrived = lax.all_to_all(whole_box, AXES, split_axis=0, concat_axis=0, tiled=True)
    return arrived.reshape(box.shape)


def body(
    winds, positions, velocity, increments, mass, requests, block_slots, destinations, cell_keys
):
    devices = lax.axis_size("lat") * lax.axis_size("lon")
    blocks = positions.shape[0]
    params = pltpu.CompilerParams(vmem_limit_bytes=40 << 20)
    smem, vmem, hbm = whole(pltpu.SMEM), whole(), whole(pltpu.HBM)
    i32, f32 = jnp.int32, jnp.float32
    dma = pltpu.SemaphoreType.DMA
    notes = [pltpu.VMEM((8, devices), i32), pltpu.SMEM((8, devices), i32)]
    by_part = (1, 0, 2)
    pos = positions.transpose(by_part)
    stay = lambda x: pltpu.with_memory_space_constraint(x, pltpu.HBM)
    others = lax.ppermute(winds, "lat", [(i, i ^ 1) for i in range(lax.axis_size("lat"))])
    both = jnp.stack([winds, others]).reshape(2 * MB, 3 * LEV, MBC)
    box, places = pl.pallas_call(
        pack_kernel,
        name="pack",
        out_shape=(
            jax.ShapeDtypeStruct((devices * ROWS, BLK), i32),
            jax.ShapeDtypeStruct((8, blocks), i32),
        ),
        in_specs=[hbm] * 6,
        out_specs=(vmem, smem),
        scratch_shapes=[
            pltpu.VMEM((1, blocks), i32),
            pltpu.VMEM((Q, devices), i32),
            pltpu.VMEM((1, blocks), i32),
            pltpu.VMEM((blocks, BLK), i32),
            pltpu.VMEM((3, blocks, BLK), f32),
            pltpu.VMEM((blocks, S, BLK), f32),
            pltpu.VMEM((2 * blocks, BLK), i32),
            pltpu.VMEM((8, blocks), i32),
            dma((7,)),
        ],
        compiler_params=params,
    )(
        stay(block_slots.transpose(1, 0)),
        stay(requests.reshape(devices, Q).transpose(1, 0)),
        stay(destinations.transpose(1, 0)),
        stay(cell_keys),
        stay(pos),
        stay(mass),
    )
    box = swap(box, devices)
    local_wind = pl.pallas_call(
        sample_kernel,
        name="sample",
        out_shape=jax.ShapeDtypeStruct((devices * WIND_ROWS, BLK), i32),
        in_specs=[vmem] * 2,
        out_specs=vmem,
        scratch_shapes=[
            pltpu.SMEM((devices * ROOM + ROOM,), i32),
            pltpu.VMEM((devices * 2 * ROOM, BLK), i32),
            *notes,
            dma,
        ],
        compiler_params=params,
    )(box, both)
    room = devices * CAP + MB + 2 * PAIR_UNROLL
    assert room + devices * CAP <= HOMES_AT and HOMES_AT + (room + devices * CAP) // 2 < PAIRS_AT
    plan, shares = pl.pallas_call(
        order_kernel,
        name="order",
        cost_estimate=pl.CostEstimate(flops=10**9, bytes_accessed=20 << 20, transcendentals=0),
        out_shape=(
            jax.ShapeDtypeStruct((PLAN,), i32),
            jax.ShapeDtypeStruct((room * S, BLK), f32),
        ),
        in_specs=[vmem],
        out_specs=(smem, vmem),
        scratch_shapes=[
            *notes,
            pltpu.SMEM((MB + 1,), i32),
            pltpu.SMEM((MB + 1,), i32),
            dma,
        ],
        compiler_params=params,
    )(box)
    returned = swap(local_wind, devices)
    drift = (pos, velocity.transpose(by_part), increments.transpose(by_part))
    row_scratch = pltpu.VMEM((blocks, BLK), i32)
    outbox = pl.pallas_call(
        height_kernel,
        name="height",
        out_shape=jax.ShapeDtypeStruct((devices * CAP, BLK), i32),
        in_specs=[smem, whole(pl.ANY)] + [vmem] * 5,
        out_specs=vmem,
        scratch_shapes=[row_scratch],
        compiler_params=params,
    )(
        places,
        plan,
        returned,
        *drift,
        cell_keys,
    )
    inbox = swap(outbox, devices)
    moved, turbulence = pl.pallas_call(
        move_kernel,
        name="move",
        out_shape=[jax.ShapeDtypeStruct(pos.shape, f32)] * 2,
        in_specs=[smem] + [vmem] * 4,
        out_specs=[vmem] * 2,
        scratch_shapes=[row_scratch, row_scratch],
        cost_estimate=pl.CostEstimate(flops=10**7, bytes_accessed=2 << 20, transcendentals=0),
        compiler_params=params,
    )(places, returned, *drift)
    total = pl.pallas_call(
        deposit_kernel,
        name="deposit",
        out_shape=jax.ShapeDtypeStruct((MB, S * LEV, MBC), f32),
        in_specs=[smem, vmem, vmem],
        out_specs=hbm,
        scratch_shapes=[pltpu.VMEM((MB, S * LEV, MBC), f32), dma((MB,))],
        compiler_params=params,
    )(plan, inbox, shares)
    return (
        moved.transpose(by_part),
        turbulence.transpose(by_part),
        total.reshape(winds.shape[:2] + (S, LEV, MBC)),
    )


def solution(mesh):
    rows = P(AXES, None, None)
    pairs = P(AXES, None)
    tiles = P("lat", "lon", None, None, None)
    return jax.shard_map(
        body,
        mesh=mesh,
        in_specs=(tiles, rows, rows, rows, rows, rows, pairs, pairs, pairs),
        out_specs=(rows, rows, tiles),
        check_vma=False,
    )
```

profile of v0, /device:TPU:1, one launch (start us, length us, event | category | flops | bytes accessed | tf_op | source)
XLA Modules:
  0.0 88.1 jit_solution(4911817638472462883)
XLA Ops:
  0.6 3.0 %pack.1 = (s32[2176,128]{1,0:T(8,128)}, s32[8,128]{1,0:T(8,128)S(1)}) custom-call(s32[1,128]{1,0:T(1,128)} %bitcast.39, s32[2,128]{1,0:T(2,128)} %bitcast.38, s32[1,128]{1,0:T(1,128)} %bitcast.40, s32[128,128]{1,0:T(8,128)} %keys.1, f32[3,128,128]{2,1,0:T(8,128)} %bitcast.27, f32[128,8,128]{2,1,0:T(8,128)} %mass_hbm.1), custom_call_target="tpu_custom_call" | custom-call | tf_op jit(solution)/shard_map/pack/pallas_call | solution.py:402
  3.6 0.0 copy-start.4
  3.7 11.5 %all-to-all-start = ((s32[2176,1,128]{2,1,0:T(1,128)}), s32[2176,1,128]{2,1,0:T(1,128)S(1)}, u32[]{:S(2)}, u32[]{:S(2)}) async-start(s32[2176,1,128]{2,1,0:T(1,128)} %bitcast.6), calls=%async_computation | async-start | bytes 2228224 | tf_op jit(solution)/shard_map/all_to_all | solution.py:383
  15.2 0.0 copy-done.4
  15.2 1.1 %collective-permute-start = (bf16[4,4,3,40,128]{4,3,2,1,0:T(8,128)(2,1)S(1)}, bf16[4,4,3,40,128]{4,3,2,1,0:T(8,128)(2,1)S(1)}, u32[]{:S(2)}, u32[]{:S(2)}) collective-permute-start(bf16[4,4,3,40,128]{4,3,2,1,0:T(8,128)(2,1)S(1)} %copy-done.4), channel_id=1, source_target_pairs={{0,16},{16,0},{32,48},{48,32},{64,80},{80,64},{96,112},{112,96},{1... | collective-permute-start | bytes 1474568 | tf_op jit(solution)/shard_map/ppermute | solution.py:400
  16.3 1.5 %collective-permute-done = bf16[4,4,3,40,128]{4,3,2,1,0:T(8,128)(2,1)S(1)} collective-permute-done((bf16[4,4,3,40,128]{4,3,2,1,0:T(8,128)(2,1)S(1)}, bf16[4,4,3,40,128]{4,3,2,1,0:T(8,128)(2,1)S(1)}, u32[]{:S(2)}, u32[]{:S(2)}) %collective-permute-start) | collective-permute-done | bytes 491552 | tf_op jit(solution)/shard_map/ppermute | solution.py:400
  17.8 0.1 pad_maximum_fusion
  17.9 16.7 %all-to-all-done = s32[2176,1,128]{2,1,0:T(1,128)S(1)} async-done(((s32[2176,1,128]{2,1,0:T(1,128)}), s32[2176,1,128]{2,1,0:T(1,128)S(1)}, u32[]{:S(2)}, u32[]{:S(2)}) %all-to-all-start) | async-done | bytes 1114144 | tf_op jit(solution)/shard_map/all_to_all | solution.py:383
  34.6 6.8 %sample.1 = s32[768,128]{1,0:T(8,128)} custom-call(s32[2176,128]{1,0:T(8,128)S(1)} %bitcast.22, bf16[32,120,128]{2,1,0:T(8,128)(2,1)S(1)} %bitcast.24), custom_call_target="tpu_custom_call" | custom-call | tf_op jit(solution)/shard_map/sample/pallas_call | solution.py:432
  41.4 7.9 %all-to-all-start.1 = ((s32[384,2,128]{2,1,0:T(2,128)}), s32[384,2,128]{2,1,0:T(2,128)S(1)}, u32[]{:S(2)}, u32[]{:S(2)}) async-start(s32[384,2,128]{2,1,0:T(2,128)} %bitcast.11), calls=%async_computation.1 | async-start | bytes 786432 | tf_op jit(solution)/shard_map/all_to_all | solution.py:383
  49.4 0.0 copy-start
  49.4 0.0 copy-start.1
  49.4 0.0 copy-start.2
  49.4 0.0 copy-start.3
  49.4 7.6 %order.1 = (s32[1024]{0:T(1024)S(1)}, f32[2432,128]{1,0:T(8,128)S(1)}) custom-call(s32[2176,128]{1,0:T(8,128)S(1)} %bitcast.23), custom_call_target="tpu_custom_call" | custom-call | flops 1000000000 | bytes 20971520 | tf_op jit(solution)/shard_map/order/pallas_call | solution.py:448
  57.0 4.9 %all-to-all-done.1 = s32[384,2,128]{2,1,0:T(2,128)S(1)} async-done(((s32[384,2,128]{2,1,0:T(2,128)}), s32[384,2,128]{2,1,0:T(2,128)S(1)}, u32[]{:S(2)}, u32[]{:S(2)}) %all-to-all-start.1) | async-done | bytes 393248 | tf_op jit(solution)/shard_map/all_to_all | solution.py:383
  62.0 0.0 copy-done
  62.0 0.0 copy-done.1
  62.0 0.0 copy-done.2
  62.0 0.0 copy-done.3
  62.0 2.1 %height.1 = s32[256,128]{1,0:T(8,128)} custom-call(s32[8,128]{1,0:T(8,128)S(1)} %get-tuple-element.9.places, s32[1024]{0:T(1024)S(1)} %get-tuple-element.13.plan, s32[768,128]{1,0:T(8,128)S(1)} %bitcast.25, f32[3,128,128]{2,1,0:T(8,128)S(1)} %bitcast.28, f32[3,128,128]{2,1,0:T(8,128)S(1)} %bitcast.30, f32[3,128,128]{2,1,0:T(8,128)S(1)} %bitcast.32, ...), custom_call_target="tpu_custom_call" | custom-call | tf_op jit(solution)/shard_map/height/pallas_call | solution.py:469
  64.1 4.2 %all-to-all-start.2 = ((s32[128,2,128]{2,1,0:T(2,128)}), s32[128,2,128]{2,1,0:T(2,128)S(1)}, u32[]{:S(2)}, u32[]{:S(2)}) async-start(s32[128,2,128]{2,1,0:T(2,128)} %bitcast.17), calls=%async_computation.2 | async-start | bytes 262144 | tf_op jit(solution)/shard_map/all_to_all | solution.py:383
  68.3 2.2 %move.1 = (f32[3,128,128]{2,1,0:T(8,128)}, f32[3,128,128]{2,1,0:T(8,128)}) custom-call(s32[8,128]{1,0:T(8,128)S(1)} %get-tuple-element.9.places, s32[768,128]{1,0:T(8,128)S(1)} %bitcast.26, f32[3,128,128]{2,1,0:T(8,128)S(1)} %bitcast.29, f32[3,128,128]{2,1,0:T(8,128)S(1)} %bitcast.31, f32[3,128,128]{2,1,0:T(8,128)S(1)} %bitcast.33), custom_call_target="tpu_custom_call" | custom-call | flops 10000000 | bytes 2097152 | tf_op jit(solution)/shard_map/move/pallas_call | solution.py:485
  70.5 7.9 %all-to-all-done.2 = s32[128,2,128]{2,1,0:T(2,128)S(1)} async-done(((s32[128,2,128]{2,1,0:T(2,128)}), s32[128,2,128]{2,1,0:T(2,128)S(1)}, u32[]{:S(2)}, u32[]{:S(2)}) %all-to-all-start.2) | async-done | bytes 131104 | tf_op jit(solution)/shard_map/all_to_all | solution.py:383
  78.4 9.7 %deposit.1 = f32[16,320,128]{2,1,0:T(8,128)} custom-call(s32[1024]{0:T(1024)S(1)} %get-tuple-element.13.plan, s32[256,128]{1,0:T(8,128)S(1)} %bitcast.34, f32[2432,128]{1,0:T(8,128)S(1)} %get-tuple-element.14.shares), custom_call_target="tpu_custom_call" | custom-call | tf_op jit(solution)/shard_map/deposit/pallas_call | solution.py:495
Async XLA Ops:
  3.6 11.5 %copy-start.4 = (bf16[4,4,3,40,128]{4,3,2,1,0:T(8,128)(2,1)S(1)}, bf16[4,4,3,40,128]{4,3,2,1,0:T(8,128)(2,1)}, u32[]{:S(2)}) copy-start(bf16[4,4,3,40,128]{4,3,2,1,0:T(8,128)(2,1)} %param.9) | copy-start | bytes 1474564
  3.7 30.9 %all-to-all-start = ((s32[2176,1,128]{2,1,0:T(1,128)}), s32[2176,1,128]{2,1,0:T(1,128)S(1)}, u32[]{:S(2)}, u32[]{:S(2)}) async-start(s32[2176,1,128]{2,1,0:T(1,128)} %bitcast.6), calls=%async_computation | async-start | bytes 2228224 | tf_op jit(solution)/shard_map/all_to_all | solution.py:383
  15.2 2.6 %collective-permute-start = (bf16[4,4,3,40,128]{4,3,2,1,0:T(8,128)(2,1)S(1)}, bf16[4,4,3,40,128]{4,3,2,1,0:T(8,128)(2,1)S(1)}, u32[]{:S(2)}, u32[]{:S(2)}) collective-permute-start(bf16[4,4,3,40,128]{4,3,2,1,0:T(8,128)(2,1)S(1)} %copy-done.4), channel_id=1, source_target_pairs={{0,16},{16,0},{32,48},{48,32},{64,80},{80,64},{96,112},{112,96},{1... | collective-permute-start | bytes 1474568 | tf_op jit(solution)/shard_map/ppermute | solution.py:400
  41.4 20.5 %all-to-all-start.1 = ((s32[384,2,128]{2,1,0:T(2,128)}), s32[384,2,128]{2,1,0:T(2,128)S(1)}, u32[]{:S(2)}, u32[]{:S(2)}) async-start(s32[384,2,128]{2,1,0:T(2,128)} %bitcast.11), calls=%async_computation.1 | async-start | bytes 786432 | tf_op jit(solution)/shard_map/all_to_all | solution.py:383
  49.4 12.6 %copy-start = (f32[128,3,128]{2,0,1:T(8,128)S(1)}, f32[128,3,128]{2,0,1:T(8,128)}, u32[]{:S(2)}) copy-start(f32[128,3,128]{2,0,1:T(8,128)} %param.10) | copy-start | bytes 589828
  49.4 12.6 %copy-start.1 = (f32[128,3,128]{2,0,1:T(8,128)S(1)}, f32[128,3,128]{2,0,1:T(8,128)}, u32[]{:S(2)}) copy-start(f32[128,3,128]{2,0,1:T(8,128)} %param.11) | copy-start | bytes 589828
  49.4 12.6 %copy-start.2 = (f32[128,3,128]{2,0,1:T(8,128)S(1)}, f32[128,3,128]{2,0,1:T(8,128)}, u32[]{:S(2)}) copy-start(f32[128,3,128]{2,0,1:T(8,128)} %param.12) | copy-start | bytes 589828
  49.4 12.6 %copy-start.3 = (s32[128,128]{1,0:T(8,128)S(1)}, s32[128,128]{1,0:T(8,128)}, u32[]{:S(2)}) copy-start(s32[128,128]{1,0:T(8,128)} %keys.1) | copy-start | bytes 196612
  64.1 14.3 %all-to-all-start.2 = ((s32[128,2,128]{2,1,0:T(2,128)}), s32[128,2,128]{2,1,0:T(2,128)S(1)}, u32[]{:S(2)}, u32[]{:S(2)}) async-start(s32[128,2,128]{2,1,0:T(2,128)} %bitcast.17), calls=%async_computation.2 | async-start | bytes 262144 | tf_op jit(solution)/shard_map/all_to_all | solution.py:383
where the time goes:
time: 88.6 us; the launch traced here: 88.1 us
  Pallas kernels  31.5 us (36%)
  waiting for transfers between devices  31 us (35%)
  starting transfers between devices  24.8 us (28%)
    all_to_all x3, waiting for transfers between devices, swap(): lax.all_to_all(whole_box, AXES, split_axis=0, concat_axis=0, tiled=True)  29.6 us
    all_to_all x3, starting transfers between devices, swap(): lax.all_to_all(whole_box, AXES, split_axis=0, concat_axis=0, tiled=True)  23.6 us
    pallas_call x1, Pallas kernels, body(): pl.pallas_call(deposit_kernel, name='deposit', out_shape=jax.ShapeDtypeSt...  9.72 us
    pallas_call x1, Pallas kernels, body(): pl.pallas_call(order_kernel, name='order', cost_estimate=pl.CostEstimate(...  7.6 us
    pallas_call x1, Pallas kernels, body(): pl.pallas_call(sample_kernel, name='sample', out_shape=jax.ShapeDtypeStru...  6.82 us
    pallas_call x1, Pallas kernels, body(): pl.pallas_call(pack_kernel, name='pack', out_shape=(jax.ShapeDtypeStruct(...  3.01 us
    pallas_call x1, Pallas kernels, body(): pl.pallas_call(move_kernel, name='move', out_shape=[jax.ShapeDtypeStruct(...  2.21 us
    pallas_call x1, Pallas kernels, body(): pl.pallas_call(height_kernel, name='height', out_shape=jax.ShapeDtypeStru...  2.1 us
  transfers between devices with their start and end apart: 4, of which 4 were waited for; matrix products, arithmetic and copies ran while one was open for 0% of the time, Pallas kernels for 11%

commit v1 on v0

--- a/solution.py
+++ b/solution.py
@@ -108,36 +108,40 @@
 
     copies[0].wait()
     slot = slots[...]
-    tile = slot // Q
+    tile = slot >> 1
     order = rank(tile)
     lons = lax.axis_size("lon")
-    core = (tile // lons) % 2
-    helper = (order + lax.axis_index("lat") + lax.axis_index("lon")) % 2
+    core = (tile >> (lons.bit_length() - 1)) & 1
+    helper = (order + lax.axis_index("lat") + lax.axis_index("lon")) & 1
     host = tile + (helper - core) * lons
-    seat = core * (ROOM // 2) + order // 2
+    seat = core * (ROOM // 2) + (order >> 1)
     copies[1].wait()
     target = targets[...]
     turn = rank(target)
     ranks[0:1, :] = host * ROWS + 2 * seat
     ranks[1:2, :] = target * ROWS + SHARE_ROW + turn * (S // 2)
     ranks[2:3, :] = host * WIND_ROWS + seat
-    ranks[3:4, :] = host * WIND_ROWS + ROOM + seat // 2
-    ranks[4:5, :] = 16 - 16 * (seat % 2)
+    ranks[3:4, :] = host * WIND_ROWS + ROOM + (seat >> 1)
+    ranks[4:5, :] = 16 - 16 * (seat & 1)
     ranks[5:6, :] = target * CAP + turn
     ranked = pltpu.make_async_copy(ranks, places, sems.at[len(copies)])
     ranked.start()
-    slot_down = stand(slot)
-    tile_down = slot_down // Q
+    bits = stand((turn << 15) | (seat << 13) | (helper << 12) | slot)
+    slot_down = bits & 0xFFF
+    helper_down = (bits >> 12) & 1
+    seat_down = (bits >> 13) & (ROOM - 1)
+    turn_down = bits >> 15
+    core_down = seat_down >> 1
     copies[2].wait()
-    met = jnp.where(slot_down % Q == 0, asked[0:1, :], asked[1:2, :])
-    met = jnp.where(tile_down == along, met, 0).astype(jnp.float32)
+    met = jnp.where((slot_down & 1) == 0, asked[0:1, :], asked[1:2, :])
+    met = jnp.where((slot_down >> 1) == along, met, 0).astype(jnp.float32)
     met = jnp.sum(met, axis=1, keepdims=True)
-    met = met + jnp.where(stand(helper) == stand(core), 0.0, float(MB))
+    met = met + jnp.where(helper_down == core_down, 0.0, float(MB))
     copies[3].wait()
-    home = (keys[:, 0:1] // MBC).astype(jnp.float32)
-    said = jnp.where(along == stand(seat), met, 0.0)
-    said = jnp.where(along == TAKEN_AT, jnp.where(stand(core) == 0, 1.0, float(EACH)), said)
-    more = jnp.where(along == HOME_AT + stand(turn), home, 0.0) + jnp.where(
+    home = (keys[:, 0:1] >> 7).astype(jnp.float32)
+    said = jnp.where(along == seat_down, met, 0.0)
+    said = jnp.where(along == TAKEN_AT, jnp.where(core_down == 0, 1.0, float(EACH)), said)
+    more = jnp.where(along == HOME_AT + turn_down, home, 0.0) + jnp.where(
         along == LANDED_AT, 1.0, 0.0
     )
     mine = jnp.concatenate([down == host, down == target], axis=1)
@@ -172,10 +176,10 @@
         taken = notes[TAKEN_AT, t]
         for r in range(ROOM // 2):
             queue[n + r] = t * ROOM + r
-        n = n + taken % EACH
+        n = n + (taken & (EACH - 1))
         for r in range(ROOM // 2):
             queue[n + r] = t * ROOM + ROOM // 2 + r
-        return n + taken // EACH
+        return n + (taken >> 3)
 
     n = lax.fori_loop(0, devices, enlist, 0, unroll=4)
     levels = lax.broadcasted_iota(jnp.int32, (LEV, BLK), 0).astype(jnp.float32)
@@ -185,7 +189,8 @@
     def step(i, _):
         for j in range(SAMPLE_UNROLL):
             item = queue[jnp.minimum(i * SAMPLE_UNROLL + j, n - 1)]
-            row = (item // ROOM) * ROWS + 2 * (item % ROOM)
+            src, seat = item >> 2, item & (ROOM - 1)
+            row = src * ROWS + 2 * seat
             yx = box[pl.ds(row, 1), :]
             height = box[pl.ds(row + 1, 1), :]
             hy = hat(upper(yx) * (1.0 / ROW_SCALE) - lats)
@@ -195,7 +200,7 @@
             flat = (hy[:, None, :] * hx[None, :, :]).reshape(MBC, BLK)
             high = flat.astype(jnp.bfloat16)
             low = (flat - high.astype(jnp.float32)).astype(jnp.bfloat16)
-            met = winds[notes[item % ROOM, item // ROOM]]
+            met = winds[notes[seat, src]]
             level_wind = jnp.dot(met, high, preferred_element_type=jnp.float32) + jnp.dot(
                 met, low, preferred_element_type=jnp.float32
             )
@@ -254,7 +259,7 @@
     n = jnp.int32(0)
     for h in range(MB):
         starts[h] = n
-        n = n + (tally[h] + 1) // 2 * 2
+        n = n + ((tally[h] + 1) & ~1)
     starts[MB] = room
 
     def place(t, _):
@@ -265,18 +270,18 @@
             at = starts[home]
             starts[home] = at + 1
             plan[at] = jnp.where(there, t * CAP + r, -1)
-            plan[HOMES_AT + at // 2] = jnp.where(there, home, 0)
+            plan[HOMES_AT + (at >> 1)] = jnp.where(there, home, 0)
         return 0
 
     lax.fori_loop(0, devices, place, 0, unroll=4)
-    plan[PAIRS_AT] = n // 2
+    plan[PAIRS_AT] = n >> 1
 
     def expand(i, _):
         for j in range(2 * PAIR_UNROLL):
             at = i * 2 * PAIR_UNROLL + j
             item = plan[at]
             row = jnp.maximum(item, 0)
-            packed = box[pl.ds((row // CAP) * ROWS + SHARE_ROW + (row % CAP) * (S // 2), S // 2), :]
+            packed = box[pl.ds((row >> 1) * ROWS + SHARE_ROW + (row & 1) * (S // 2), S // 2), :]
             unit = jnp.where(item < 0, 0.0, 1.0 / M_SCALE)
             shares[pl.ds(S * at, S), :] = (
                 jnp.concatenate([upper(packed), lower(packed)], axis=0) * unit

time: 88.6 us -> 87.8 us (level); the launches traced: 88.1 us -> 89.3 us
  starting transfers between devices: 24.8 us -> 22 us
  Pallas kernels: 31.5 us -> 33.7 us
  waiting for transfers between devices: 31 us -> 32.7 us
    pallas_call x1, Pallas kernels: 6.82 us -> 10.6 us  [body(): pl.pallas_call(sample_kernel, name='sample', out_shape=jax.ShapeDtypeStru...]
    all_to_all x3, starting transfers between devices: 23.6 us -> 20.9 us  [swap(): lax.all_to_all(whole_box, AXES, split_axis=0, concat_axis=0, tiled=True)]
    all_to_all x3, waiting for transfers between devices: 29.6 us -> 31.2 us  [swap(): lax.all_to_all(whole_box, AXES, split_axis=0, concat_axis=0, tiled=True)]
    pallas_call x1, Pallas kernels: 7.6 us -> 6.06 us  [body(): pl.pallas_call(order_kernel, name='order', cost_estimate=pl.CostEstimate(...]
  transfers between devices with their start and end apart: 4 -> 4, of which waited for: 4 -> 4; matrix products, arithmetic and copies ran while one was open for 0% -> 0% of each run, Pallas kernels for 11% -> 9%
where the time goes in v1:
time: 87.8 us; the launch traced here: 89.3 us
  Pallas kernels  33.7 us (38%)
  waiting for transfers between devices  32.7 us (37%)
  starting transfers between devices  22 us (25%)
    all_to_all x3, waiting for transfers between devices, swap(): lax.all_to_all(whole_box, AXES, split_axis=0, concat_axis=0, tiled=True)  31.2 us
    all_to_all x3, starting transfers between devices, swap(): lax.all_to_all(whole_box, AXES, split_axis=0, concat_axis=0, tiled=True)  20.9 us
    pallas_call x1, Pallas kernels, body(): pl.pallas_call(sample_kernel, name='sample', out_shape=jax.ShapeDtypeStru...  10.6 us
    pallas_call x1, Pallas kernels, body(): pl.pallas_call(deposit_kernel, name='deposit', out_shape=jax.ShapeDtypeSt...  9.7 us
    pallas_call x1, Pallas kernels, body(): pl.pallas_call(order_kernel, name='order', cost_estimate=pl.CostEstimate(...  6.06 us
    pallas_call x1, Pallas kernels, body(): pl.pallas_call(pack_kernel, name='pack', out_shape=(jax.ShapeDtypeStruct(...  2.98 us
    pallas_call x1, Pallas kernels, body(): pl.pallas_call(move_kernel, name='move', out_shape=[jax.ShapeDtypeStruct(...  2.21 us
    pallas_call x1, Pallas kernels, body(): pl.pallas_call(height_kernel, name='height', out_shape=jax.ShapeDtypeStru...  2.1 us
  transfers between devices with their start and end apart: 4, of which 4 were waited for; matrix products, arithmetic and copies ran while one was open for 0% of the time, Pallas kernels for 9%

profile of v1, /device:TPU:1, one launch (start us, length us, event | category | flops | bytes accessed | tf_op | source)
XLA Modules:
  0.0 89.3 jit_solution(4177758985429194915)
XLA Ops:
  0.6 3.0 %pack.1 = (s32[2176,128]{1,0:T(8,128)}, s32[8,128]{1,0:T(8,128)S(1)}) custom-call(s32[1,128]{1,0:T(1,128)} %bitcast.39, s32[2,128]{1,0:T(2,128)} %bitcast.38, s32[1,128]{1,0:T(1,128)} %bitcast.40, s32[128,128]{1,0:T(8,128)} %keys.1, f32[3,128,128]{2,1,0:T(8,128)} %bitcast.27, f32[128,8,128]{2,1,0:T(8,128)} %mass_hbm.1), custom_call_target="tpu_custom_call" | custom-call | tf_op jit(solution)/shard_map/pack/pallas_call | solution.py:407
  3.6 0.0 copy-start.4
  3.6 11.5 %all-to-all-start = ((s32[2176,1,128]{2,1,0:T(1,128)}), s32[2176,1,128]{2,1,0:T(1,128)S(1)}, u32[]{:S(2)}, u32[]{:S(2)}) async-start(s32[2176,1,128]{2,1,0:T(1,128)} %bitcast.6), calls=%async_computation | async-start | bytes 2228224 | tf_op jit(solution)/shard_map/all_to_all | solution.py:388
  15.1 0.0 copy-done.4
  15.1 1.1 %collective-permute-start = (bf16[4,4,3,40,128]{4,3,2,1,0:T(8,128)(2,1)S(1)}, bf16[4,4,3,40,128]{4,3,2,1,0:T(8,128)(2,1)S(1)}, u32[]{:S(2)}, u32[]{:S(2)}) collective-permute-start(bf16[4,4,3,40,128]{4,3,2,1,0:T(8,128)(2,1)S(1)} %copy-done.4), channel_id=1, source_target_pairs={{0,16},{16,0},{32,48},{48,32},{64,80},{80,64},{96,112},{112,96},{1... | collective-permute-start | bytes 1474568 | tf_op jit(solution)/shard_map/ppermute | solution.py:405
  16.3 1.5 %collective-permute-done = bf16[4,4,3,40,128]{4,3,2,1,0:T(8,128)(2,1)S(1)} collective-permute-done((bf16[4,4,3,40,128]{4,3,2,1,0:T(8,128)(2,1)S(1)}, bf16[4,4,3,40,128]{4,3,2,1,0:T(8,128)(2,1)S(1)}, u32[]{:S(2)}, u32[]{:S(2)}) %collective-permute-start) | collective-permute-done | bytes 491552 | tf_op jit(solution)/shard_map/ppermute | solution.py:405
  17.8 0.1 pad_maximum_fusion
  17.9 16.7 %all-to-all-done = s32[2176,1,128]{2,1,0:T(1,128)S(1)} async-done(((s32[2176,1,128]{2,1,0:T(1,128)}), s32[2176,1,128]{2,1,0:T(1,128)S(1)}, u32[]{:S(2)}, u32[]{:S(2)}) %all-to-all-start) | async-done | bytes 1114144 | tf_op jit(solution)/shard_map/all_to_all | solution.py:388
  34.6 10.6 %sample.1 = s32[768,128]{1,0:T(8,128)} custom-call(s32[2176,128]{1,0:T(8,128)S(1)} %bitcast.22, bf16[32,120,128]{2,1,0:T(8,128)(2,1)S(1)} %bitcast.24), custom_call_target="tpu_custom_call" | custom-call | tf_op jit(solution)/shard_map/sample/pallas_call | solution.py:437
  45.2 5.2 %all-to-all-start.1 = ((s32[384,2,128]{2,1,0:T(2,128)}), s32[384,2,128]{2,1,0:T(2,128)S(1)}, u32[]{:S(2)}, u32[]{:S(2)}) async-start(s32[384,2,128]{2,1,0:T(2,128)} %bitcast.11), calls=%async_computation.1 | async-start | bytes 786432 | tf_op jit(solution)/shard_map/all_to_all | solution.py:388
  50.4 0.0 copy-start
  50.4 0.0 copy-start.1
  50.5 0.0 copy-start.2
  50.5 0.0 copy-start.3
  50.5 6.1 %order.1 = (s32[1024]{0:T(1024)S(1)}, f32[2432,128]{1,0:T(8,128)S(1)}) custom-call(s32[2176,128]{1,0:T(8,128)S(1)} %bitcast.23), custom_call_target="tpu_custom_call" | custom-call | flops 1000000000 | bytes 20971520 | tf_op jit(solution)/shard_map/order/pallas_call | solution.py:453
  56.6 6.6 %all-to-all-done.1 = s32[384,2,128]{2,1,0:T(2,128)S(1)} async-done(((s32[384,2,128]{2,1,0:T(2,128)}), s32[384,2,128]{2,1,0:T(2,128)S(1)}, u32[]{:S(2)}, u32[]{:S(2)}) %all-to-all-start.1) | async-done | bytes 393248 | tf_op jit(solution)/shard_map/all_to_all | solution.py:388
  63.2 0.0 copy-done
  63.2 0.0 copy-done.1
  63.2 0.0 copy-done.2
  63.2 0.0 copy-done.3
  63.2 2.1 %height.1 = s32[256,128]{1,0:T(8,128)} custom-call(s32[8,128]{1,0:T(8,128)S(1)} %get-tuple-element.9.places, s32[1024]{0:T(1024)S(1)} %get-tuple-element.13.plan, s32[768,128]{1,0:T(8,128)S(1)} %bitcast.25, f32[3,128,128]{2,1,0:T(8,128)S(1)} %bitcast.28, f32[3,128,128]{2,1,0:T(8,128)S(1)} %bitcast.30, f32[3,128,128]{2,1,0:T(8,128)S(1)} %bitcast.32, ...), custom_call_target="tpu_custom_call" | custom-call | tf_op jit(solution)/shard_map/height/pallas_call | solution.py:474
  65.3 4.2 %all-to-all-start.2 = ((s32[128,2,128]{2,1,0:T(2,128)}), s32[128,2,128]{2,1,0:T(2,128)S(1)}, u32[]{:S(2)}, u32[]{:S(2)}) async-start(s32[128,2,128]{2,1,0:T(2,128)} %bitcast.17), calls=%async_computation.2 | async-start | bytes 262144 | tf_op jit(solution)/shard_map/all_to_all | solution.py:388
  69.5 2.2 %move.1 = (f32[3,128,128]{2,1,0:T(8,128)}, f32[3,128,128]{2,1,0:T(8,128)}) custom-call(s32[8,128]{1,0:T(8,128)S(1)} %get-tuple-element.9.places, s32[768,128]{1,0:T(8,128)S(1)} %bitcast.26, f32[3,128,128]{2,1,0:T(8,128)S(1)} %bitcast.29, f32[3,128,128]{2,1,0:T(8,128)S(1)} %bitcast.31, f32[3,128,128]{2,1,0:T(8,128)S(1)} %bitcast.33), custom_call_target="tpu_custom_call" | custom-call | flops 10000000 | bytes 2097152 | tf_op jit(solution)/shard_map/move/pallas_call | solution.py:490
  71.7 7.9 %all-to-all-done.2 = s32[128,2,128]{2,1,0:T(2,128)S(1)} async-done(((s32[128,2,128]{2,1,0:T(2,128)}), s32[128,2,128]{2,1,0:T(2,128)S(1)}, u32[]{:S(2)}, u32[]{:S(2)}) %all-to-all-start.2) | async-done | bytes 131104 | tf_op jit(solution)/shard_map/all_to_all | solution.py:388
  79.6 9.7 %deposit.1 = f32[16,320,128]{2,1,0:T(8,128)} custom-call(s32[1024]{0:T(1024)S(1)} %get-tuple-element.13.plan, s32[256,128]{1,0:T(8,128)S(1)} %bitcast.34, f32[2432,128]{1,0:T(8,128)S(1)} %get-tuple-element.14.shares), custom_call_target="tpu_custom_call" | custom-call | tf_op jit(solution)/shard_map/deposit/pallas_call | solution.py:500
Async XLA Ops:
  3.6 11.5 %copy-start.4 = (bf16[4,4,3,40,128]{4,3,2,1,0:T(8,128)(2,1)S(1)}, bf16[4,4,3,40,128]{4,3,2,1,0:T(8,128)(2,1)}, u32[]{:S(2)}) copy-start(bf16[4,4,3,40,128]{4,3,2,1,0:T(8,128)(2,1)} %param.9) | copy-start | bytes 1474564
  3.6 30.9 %all-to-all-start = ((s32[2176,1,128]{2,1,0:T(1,128)}), s32[2176,1,128]{2,1,0:T(1,128)S(1)}, u32[]{:S(2)}, u32[]{:S(2)}) async-start(s32[2176,1,128]{2,1,0:T(1,128)} %bitcast.6), calls=%async_computation | async-start | bytes 2228224 | tf_op jit(solution)/shard_map/all_to_all | solution.py:388
  15.1 2.6 %collective-permute-start = (bf16[4,4,3,40,128]{4,3,2,1,0:T(8,128)(2,1)S(1)}, bf16[4,4,3,40,128]{4,3,2,1,0:T(8,128)(2,1)S(1)}, u32[]{:S(2)}, u32[]{:S(2)}) collective-permute-start(bf16[4,4,3,40,128]{4,3,2,1,0:T(8,128)(2,1)S(1)} %copy-done.4), channel_id=1, source_target_pairs={{0,16},{16,0},{32,48},{48,32},{64,80},{80,64},{96,112},{112,96},{1... | collective-permute-start | bytes 1474568 | tf_op jit(solution)/shard_map/ppermute | solution.py:405
  45.2 17.9 %all-to-all-start.1 = ((s32[384,2,128]{2,1,0:T(2,128)}), s32[384,2,128]{2,1,0:T(2,128)S(1)}, u32[]{:S(2)}, u32[]{:S(2)}) async-start(s32[384,2,128]{2,1,0:T(2,128)} %bitcast.11), calls=%async_computation.1 | async-start | bytes 786432 | tf_op jit(solution)/shard_map/all_to_all | solution.py:388
  50.4 12.7 %copy-start = (f32[128,3,128]{2,0,1:T(8,128)S(1)}, f32[128,3,128]{2,0,1:T(8,128)}, u32[]{:S(2)}) copy-start(f32[128,3,128]{2,0,1:T(8,128)} %param.10) | copy-start | bytes 589828
  50.4 12.7 %copy-start.1 = (f32[128,3,128]{2,0,1:T(8,128)S(1)}, f32[128,3,128]{2,0,1:T(8,128)}, u32[]{:S(2)}) copy-start(f32[128,3,128]{2,0,1:T(8,128)} %param.11) | copy-start | bytes 589828
  50.5 12.7 %copy-start.2 = (f32[128,3,128]{2,0,1:T(8,128)S(1)}, f32[128,3,128]{2,0,1:T(8,128)}, u32[]{:S(2)}) copy-start(f32[128,3,128]{2,0,1:T(8,128)} %param.12) | copy-start | bytes 589828
  50.5 12.7 %copy-start.3 = (s32[128,128]{1,0:T(8,128)S(1)}, s32[128,128]{1,0:T(8,128)}, u32[]{:S(2)}) copy-start(s32[128,128]{1,0:T(8,128)} %keys.1) | copy-start | bytes 196612
  65.3 14.3 %all-to-all-start.2 = ((s32[128,2,128]{2,1,0:T(2,128)}), s32[128,2,128]{2,1,0:T(2,128)S(1)}, u32[]{:S(2)}, u32[]{:S(2)}) async-start(s32[128,2,128]{2,1,0:T(2,128)} %bitcast.17), calls=%async_computation.2 | async-start | bytes 262144 | tf_op jit(solution)/shard_map/all_to_all | solution.py:388
